TPU v7x, 256 devices: a whole 4x4x8 slice. The times are simulated.
256 devices in a mesh: tm: 64 (over y_hi, x, z), space: 4 (over y_lo, core).
Axes of the slice: x: 4, y: 4 (y_hi: 2, y_lo: 2; y = y_hi * 2 + y_lo), z: 8, core: 2. Of those that a mesh axis runs over, the one named last changes fastest.
Arguments:
- guess: float32 [64, 1024, 1024], P('tm', 'space'), may hold values from -2.5 to 2.5
- kappa: float32 [1024, 1024], P('space'), may hold values from 0.25 to 1
- rate: float32 [1024, 1024], P('space'), may hold values from 0.005 to 0.02
Outputs:
- c_points: float32 [64, 1024, 1024], P('tm', 'space')
- last_fine: float32 [64, 1024, 1024], P('tm', 'space')
All inputs are finite; a program needn't handle non-finite values.
Results may differ from a plain program's by a relative error of at most 0.00002.
Values sent between devices are 32-bit elements; how exact they have to be, the bound alone decides.
No kernel may reach another device: no remote copies, remote signals or barrier semaphores. Data moves between devices by JAX's collectives and lax.ppermute only.
A program may use at most 64 MiB of HBM per device.

v0:
```python
import jax
import jax.numpy as jnp
from jax import lax
from jax.sharding import PartitionSpec as P

STEPS = 4
GROUP = 4
SWEEPS = 2


DIFFUSION = 0.05


def extended(shard, sides, width):
    for axis, dim in sides:
        peers, length = (lax.axis_size(axis), shard.shape[dim])
        up = [(i, (i + 1) % peers) for i in range(peers - 1)]
        down = [(j, i) for i, j in up]
        last = lax.slice_in_dim(shard, length - width, length, axis=dim)
        initial = lax.slice_in_dim(shard, 0, width, axis=dim)
        before = lax.ppermute(last, axis, up)
        after = lax.ppermute(initial, axis, down)
        shard = jnp.concatenate([before, shard, after], axis=dim)
    return shard


def from_behind(value, axis, steps):
    count = lax.axis_size(axis)
    initial, last = (max(0, -steps), min(count, count - steps))
    return lax.ppermute(value, axis, [(source, source + steps) for source in range(initial, last)])


def advance_padded(padded, kappa, rate, scale):
    centre = padded[1:-1, 1:-1]
    laplace = (
        padded[2:, 1:-1] + padded[:-2, 1:-1] + padded[1:-1, 2:] + padded[1:-1, :-2] - 4.0 * centre
    )
    return centre + scale * (
        DIFFUSION * kappa * laplace + rate * (centre - centre * centre * centre)
    )


def deep_border(state, count):
    return extended(state, (("space", 0),), count)


def deep_step(wide, margin, widened, scale):
    rows = widened.shape[1] - 2 * STEPS
    height = wide.shape[0] - 2
    lower = STEPS - (margin - 1)
    kappa_rows = widened[0, lower : lower + height]
    rate_rows = widened[1, lower : lower + height]
    stepped = advance_padded(jnp.pad(wide, ((0, 0), (1, 1))), kappa_rows, rate_rows, scale)
    strip = lax.axis_index("space")
    total = rows * lax.axis_size("space")
    global_rows = strip * rows - (margin - 1) + lax.broadcasted_iota(jnp.int32, stepped.shape, 0)
    inside = (global_rows >= 0) & (global_rows < total)
    return jnp.where(inside, stepped, jnp.zeros_like(stepped))


def deep_march(wide, margin, widened, count):
    for repeat in range(count):
        wide = deep_step(wide, margin, widened, 1.0)
        margin = margin - 1
    return wide


def forward(state):
    return from_behind(state, "tm", 1)


def local(guess, kappa, rate):
    position = lax.axis_index("tm")
    member = position % GROUP
    coarse_scale = float(STEPS)
    state = guess[0]
    incoming = forward(state)
    widened = extended(jnp.stack([kappa, rate]), (("space", 1),), STEPS)
    marched = deep_march(deep_border(incoming, STEPS), STEPS, widened, STEPS)
    relaxed = jnp.where(position == 0, state, marched)
    incoming = forward(relaxed)
    wide = deep_border(incoming, STEPS)
    rows = relaxed.shape[0]
    band = jnp.pad(wide[STEPS - 1 : STEPS + rows + 1], ((0, 0), (1, 1)))
    coarse_image = advance_padded(band, kappa, rate, coarse_scale)
    fine_image = deep_march(wide, STEPS, widened, STEPS)
    defect = jnp.where(position == 0, jnp.zeros_like(fine_image), fine_image - coarse_image)
    coarse = relaxed
    for sweep_number in range(SWEEPS):
        for turn in range(GROUP):
            arrived = from_behind(coarse, "tm", 1)
            framed = extended(arrived, (("space", 0),), 1)
            framed = jnp.pad(framed, ((0, 0), (1, 1)))
            updated = advance_padded(framed, kappa, rate, coarse_scale) + defect
            if turn + 1 < GROUP:
                active = member == turn + 1
            else:
                active = (member == 0) & (position >= GROUP)
            coarse = jnp.where(active, updated, coarse)
    last_fine = deep_march(deep_border(coarse, STEPS - 1), STEPS - 1, widened, STEPS - 1)
    return (coarse[None], last_fine[None])


def solution(mesh):
    return jax.shard_map(
        local,
        mesh=mesh,
        in_specs=(P("tm", "space", None), P("space", None), P("space", None)),
        out_specs=(P("tm", "space", None), P("tm", "space", None)),
        check_vma=False,
    )
```

profile of v0, /device:TPU:17, one launch (start us, length us, event | category | flops | bytes accessed | tf_op | source)
XLA Modules:
  0.0 411.9 jit_solution(17680369697969683800)
XLA Ops:
  0.6 3.5 collective-permute-start
  5.1 3.8 collective-permute-start.3
  10.9 22.3 %collective-permute-done = f32[256,1024]{1,0:T(8,128)S(1)} collective-permute-done((f32[256,1024]{1,0:T(8,128)}, f32[256,1024]{1,0:T(8,128)S(1)}, u32[]{:S(2)}, u32[]{:S(2)}) %collective-permute-start) | collective-permute-done | bytes 1048608 | tf_op jit(solution)/shard_map/ppermute | solution.py:30
  33.2 5.0 %collective-permute-start.1 = (f32[4,1024]{1,0:T(4,128)S(1)}, f32[4,1024]{1,0:T(4,128)S(1)}, u32[]{:S(2)}, u32[]{:S(2)}) collective-permute-start(f32[4,1024]{1,0:T(4,128)S(1)} %get-tuple-element.26), channel_id=1, source_target_pairs={{0,1},{1,2},{2,3},{4,5},{5,6},{6,7},{8,9},{9,10},{10,11},{12,13},{... | collective-permute-start | bytes 49160 | tf_op jit(solution)/shard_map/ppermute | solution.py:21
  47.4 2.1 fusion.75
  51.4 29.5 %collective-permute-done.5 = f32[256,1024]{1,0:T(8,128)} collective-permute-done((f32[256,1024]{1,0:T(8,128)}, f32[256,1024]{1,0:T(8,128)}, u32[]{:S(2)}, u32[]{:S(2)}) %collective-permute-start.5) | collective-permute-done | bytes 1048608 | tf_op jit(solution)/shard_map/ppermute | solution.py:30
  83.6 3.6 collective-permute-start.7
  90.0 2.6 collective-permute-start.9
  100.2 7.0 %fusion.174 = (f32[256,1024]{1,0:T(8,128)S(1)}, f32[256,1024]{1,0:T(8,128)}) fusion(f32[256,1024]{1,0:T(8,128)} %fusion.75, f32[256,1024]{1,0:T(8,128)} %collective-permute-done.5, f32[258,1026]{1,0:T(8,128)S(1)} %select_maximum_fusion.14, f32[1,1024]{1,0:T(1,128)S(1)} %collective-permute-done.7, f32[1,1024]{1,0:T(1,128)S(1)} %collective-permute-done.6, ...), kind=kLoop, calls=%fused_computation.286 | loop fusion | flops 11272192 | bytes 13738498 | tf_op jit(solution)/shard_map/jit(_where)/select_n | solution.py:99
  109.1 29.7 %collective-permute-done.10 = f32[256,1024]{1,0:T(8,128)S(1)} collective-permute-done((f32[256,1024]{1,0:T(8,128)S(1)}, f32[256,1024]{1,0:T(8,128)S(1)}, u32[]{:S(2)}, u32[]{:S(2)}) %collective-permute-start.10) | collective-permute-done | bytes 1048608 | tf_op jit(solution)/shard_map/ppermute | solution.py:30
  141.8 3.6 collective-permute-start.12
  147.8 3.5 fusion.108
  151.3 1.9 collective-permute-start.13
  153.2 29.9 %collective-permute-done.13 = f32[256,1024]{1,0:T(8,128)S(1)} collective-permute-done((f32[256,1024]{1,0:T(8,128)S(1)}, f32[256,1024]{1,0:T(8,128)S(1)}, u32[]{:S(2)}, u32[]{:S(2)}) %collective-permute-start.13) | collective-permute-done | bytes 1048608 | tf_op jit(solution)/shard_map/ppermute | solution.py:30
  186.1 3.6 collective-permute-start.15
  192.1 3.5 fusion.114
  197.5 29.9 %collective-permute-done.16 = f32[256,1024]{1,0:T(8,128)S(1)} collective-permute-done((f32[256,1024]{1,0:T(8,128)S(1)}, f32[256,1024]{1,0:T(8,128)S(1)}, u32[]{:S(2)}, u32[]{:S(2)}) %collective-permute-start.16) | collective-permute-done | bytes 1048608 | tf_op jit(solution)/shard_map/ppermute | solution.py:30
  228.5 1.9 collective-permute-start.17
  230.4 3.6 collective-permute-start.18
  236.5 3.2 fusion.120
  239.7 2.1 collective-permute-start.19
  241.8 29.7 %collective-permute-done.19 = f32[256,1024]{1,0:T(8,128)S(1)} collective-permute-done((f32[256,1024]{1,0:T(8,128)S(1)}, f32[256,1024]{1,0:T(8,128)S(1)}, u32[]{:S(2)}, u32[]{:S(2)}) %collective-permute-start.19) | collective-permute-done | bytes 1048608 | tf_op jit(solution)/shard_map/ppermute | solution.py:30
  273.4 3.6 collective-permute-start.21
  281.2 29.9 %collective-permute-done.22 = f32[256,1024]{1,0:T(8,128)S(1)} collective-permute-done((f32[256,1024]{1,0:T(8,128)S(1)}, f32[256,1024]{1,0:T(8,128)S(1)}, u32[]{:S(2)}, u32[]{:S(2)}) %collective-permute-start.22) | collective-permute-done | bytes 1048608 | tf_op jit(solution)/shard_map/ppermute | solution.py:30
  313.0 3.6 collective-permute-start.24
  320.7 29.9 %collective-permute-done.25 = f32[256,1024]{1,0:T(8,128)S(1)} collective-permute-done((f32[256,1024]{1,0:T(8,128)S(1)}, f32[256,1024]{1,0:T(8,128)S(1)}, u32[]{:S(2)}, u32[]{:S(2)}) %collective-permute-start.25) | collective-permute-done | bytes 1048608 | tf_op jit(solution)/shard_map/ppermute | solution.py:30
  352.5 3.6 collective-permute-start.27
  360.3 29.9 %collective-permute-done.28 = f32[256,1024]{1,0:T(8,128)S(1)} collective-permute-done((f32[256,1024]{1,0:T(8,128)S(1)}, f32[256,1024]{1,0:T(8,128)S(1)}, u32[]{:S(2)}, u32[]{:S(2)}) %collective-permute-start.28) | collective-permute-done | bytes 1048608 | tf_op jit(solution)/shard_map/ppermute | solution.py:30
  392.1 3.6 collective-permute-start.30
  397.9 4.2 %collective-permute-start.31 = (f32[3,1024]{1,0:T(4,128)S(1)}, f32[3,1024]{1,0:T(4,128)S(1)}, u32[]{:S(2)}, u32[]{:S(2)}) collective-permute-start(f32[3,1024]{1,0:T(4,128)S(1)} %get-tuple-element.6), channel_id=1, source_target_pairs={{0,1},{1,2},{2,3},{4,5},{5,6},{6,7},{8,9},{9,10},{10,11},{12,13},{... | collective-permute-start | bytes 36872 | tf_op jit(solution)/shard_map/ppermute | solution.py:21
  404.0 3.1 collective-permute-done.32
  409.8 2.1 fusion.99
  (119 shorter events, 71.1 us)
Async XLA Ops:
  0.6 32.5 %collective-permute-start = (f32[256,1024]{1,0:T(8,128)}, f32[256,1024]{1,0:T(8,128)S(1)}, u32[]{:S(2)}, u32[]{:S(2)}) collective-permute-start(f32[256,1024]{1,0:T(8,128)} %bitcast.56), channel_id=1, source_target_pairs={{0,4},{4,8},{8,12},{12,16},{16,20},{20,24},{24,28},{28,32},{32,36}... | collective-permute-start | bytes 3145736 | tf_op jit(solution)/shard_map/ppermute | solution.py:30
  5.1 35.0 %collective-permute-start.3 = (f32[2,4,1024]{2,1,0:T(4,128)S(1)}, f32[2,4,1024]{2,1,0:T(4,128)S(1)}, u32[]{:S(2)}, u32[]{:S(2)}) collective-permute-start(f32[2,4,1024]{2,1,0:T(4,128)S(1)} %get-tuple-element.4), channel_id=1, source_target_pairs={{0,1},{1,2},{2,3},{4,5},{5,6},{6,7},{8,9},{9,10},{10,11},{12,13},{... | collective-permute-start | bytes 98312 | tf_op jit(solution)/shard_map/ppermute | solution.py:21
  8.9 31.3 %collective-permute-start.4 = (f32[2,4,1024]{2,1,0:T(4,128)S(1)}, f32[2,4,1024]{2,1,0:T(4,128)S(1)}, u32[]{:S(2)}, u32[]{:S(2)}) collective-permute-start(f32[2,4,1024]{2,1,0:T(4,128)S(1)} %get-tuple-element.5), channel_id=1, source_target_pairs={{1,0},{2,1},{3,2},{5,4},{6,5},{7,6},{9,8},{10,9},{11,10},{13,12},{... | collective-permute-start | bytes 98312 | tf_op jit(solution)/shard_map/ppermute | solution.py:22
  33.2 8.8 %collective-permute-start.1 = (f32[4,1024]{1,0:T(4,128)S(1)}, f32[4,1024]{1,0:T(4,128)S(1)}, u32[]{:S(2)}, u32[]{:S(2)}) collective-permute-start(f32[4,1024]{1,0:T(4,128)S(1)} %get-tuple-element.26), channel_id=1, source_target_pairs={{0,1},{1,2},{2,3},{4,5},{5,6},{6,7},{8,9},{9,10},{10,11},{12,13},{... | collective-permute-start | bytes 49160 | tf_op jit(solution)/shard_map/ppermute | solution.py:21
  38.2 5.1 %collective-permute-start.2 = (f32[4,1024]{1,0:T(4,128)S(1)}, f32[4,1024]{1,0:T(4,128)S(1)}, u32[]{:S(2)}, u32[]{:S(2)}) collective-permute-start(f32[4,1024]{1,0:T(4,128)S(1)} %get-tuple-element.27), channel_id=1, source_target_pairs={{1,0},{2,1},{3,2},{5,4},{6,5},{7,6},{9,8},{10,9},{11,10},{13,12},{... | collective-permute-start | bytes 49160 | tf_op jit(solution)/shard_map/ppermute | solution.py:22
  49.5 31.4 %collective-permute-start.5 = (f32[256,1024]{1,0:T(8,128)}, f32[256,1024]{1,0:T(8,128)}, u32[]{:S(2)}, u32[]{:S(2)}) collective-permute-start(f32[256,1024]{1,0:T(8,128)} %fusion.75), channel_id=1, source_target_pairs={{0,4},{4,8},{8,12},{12,16},{16,20},{20,24},{24,28},{28,32},{32,36}... | collective-permute-start | bytes 3145736 | tf_op jit(solution)/shard_map/ppermute | solution.py:30
  81.7 10.9 %collective-permute-start.6 = (f32[1,1024]{1,0:T(1,128)S(1)}, f32[1,1024]{1,0:T(1,128)S(1)}, u32[]{:S(2)}, u32[]{:S(2)}) collective-permute-start(f32[1,1024]{1,0:T(1,128)S(1)} %get-tuple-element.25), channel_id=1, source_target_pairs={{1,0},{2,1},{3,2},{5,4},{6,5},{7,6},{9,8},{10,9},{11,10},{13,12},{... | collective-permute-start | bytes 12296 | tf_op jit(solution)/shard_map/ppermute | solution.py:22
  83.6 9.0 %collective-permute-start.7 = (f32[1,1024]{1,0:T(1,128)S(1)}, f32[1,1024]{1,0:T(1,128)S(1)}, u32[]{:S(2)}, u32[]{:S(2)}) collective-permute-start(f32[1,1024]{1,0:T(1,128)S(1)} %get-tuple-element.24), channel_id=1, source_target_pairs={{0,1},{1,2},{2,3},{4,5},{5,6},{6,7},{8,9},{9,10},{10,11},{12,13},{... | collective-permute-start | bytes 12296 | tf_op jit(solution)/shard_map/ppermute | solution.py:21
  88.0 6.2 %collective-permute-start.8 = (f32[4,1024]{1,0:T(4,128)S(1)}, f32[4,1024]{1,0:T(4,128)S(1)}, u32[]{:S(2)}, u32[]{:S(2)}) collective-permute-start(f32[4,1024]{1,0:T(4,128)S(1)} %get-tuple-element.22), channel_id=1, source_target_pairs={{0,1},{1,2},{2,3},{4,5},{5,6},{6,7},{8,9},{9,10},{10,11},{12,13},{... | collective-permute-start | bytes 49160 | tf_op jit(solution)/shard_map/ppermute | solution.py:21
  90.0 5.1 %collective-permute-start.9 = (f32[4,1024]{1,0:T(4,128)S(1)}, f32[4,1024]{1,0:T(4,128)S(1)}, u32[]{:S(2)}, u32[]{:S(2)}) collective-permute-start(f32[4,1024]{1,0:T(4,128)S(1)} %get-tuple-element.23), channel_id=1, source_target_pairs={{1,0},{2,1},{3,2},{5,4},{6,5},{7,6},{9,8},{10,9},{11,10},{13,12},{... | collective-permute-start | bytes 49160 | tf_op jit(solution)/shard_map/ppermute | solution.py:22
  107.2 31.6 %collective-permute-start.10 = (f32[256,1024]{1,0:T(8,128)S(1)}, f32[256,1024]{1,0:T(8,128)S(1)}, u32[]{:S(2)}, u32[]{:S(2)}) collective-permute-start(f32[256,1024]{1,0:T(8,128)S(1)} %get-tuple-element.2), channel_id=1, source_target_pairs={{0,4},{4,8},{8,12},{12,16},{16,20},{20,24},{24,28},{28,32},{32,36}... | collective-permute-start | bytes 3145736 | tf_op jit(solution)/shard_map/ppermute | solution.py:30
  139.8 5.6 %collective-permute-start.11 = (f32[1,1024]{1,0:T(1,128)S(1)}, f32[1,1024]{1,0:T(1,128)S(1)}, u32[]{:S(2)}, u32[]{:S(2)}) collective-permute-start(f32[1,1024]{1,0:T(1,128)S(1)} %get-tuple-element.21), channel_id=1, source_target_pairs={{1,0},{2,1},{3,2},{5,4},{6,5},{7,6},{9,8},{10,9},{11,10},{13,12},{... | collective-permute-start | bytes 12296 | tf_op jit(solution)/shard_map/ppermute | solution.py:22
  141.8 4.4 %collective-permute-start.12 = (f32[1,1024]{1,0:T(1,128)S(1)}, f32[1,1024]{1,0:T(1,128)S(1)}, u32[]{:S(2)}, u32[]{:S(2)}) collective-permute-start(f32[1,1024]{1,0:T(1,128)S(1)} %get-tuple-element.20), channel_id=1, source_target_pairs={{0,1},{1,2},{2,3},{4,5},{5,6},{6,7},{8,9},{9,10},{10,11},{12,13},{... | collective-permute-start | bytes 12296 | tf_op jit(solution)/shard_map/ppermute | solution.py:21
  151.3 31.9 %collective-permute-start.13 = (f32[256,1024]{1,0:T(8,128)S(1)}, f32[256,1024]{1,0:T(8,128)S(1)}, u32[]{:S(2)}, u32[]{:S(2)}) collective-permute-start(f32[256,1024]{1,0:T(8,128)S(1)} %fusion.108), channel_id=1, source_target_pairs={{0,4},{4,8},{8,12},{12,16},{16,20},{20,24},{24,28},{28,32},{32,36}... | collective-permute-start | bytes 3145736 | tf_op jit(solution)/shard_map/ppermute | solution.py:30
  184.2 5.6 %collective-permute-start.14 = (f32[1,1024]{1,0:T(1,128)S(1)}, f32[1,1024]{1,0:T(1,128)S(1)}, u32[]{:S(2)}, u32[]{:S(2)}) collective-permute-start(f32[1,1024]{1,0:T(1,128)S(1)} %get-tuple-element.19), channel_id=1, source_target_pairs={{1,0},{2,1},{3,2},{5,4},{6,5},{7,6},{9,8},{10,9},{11,10},{13,12},{... | collective-permute-start | bytes 12296 | tf_op jit(solution)/shard_map/ppermute | solution.py:22
  186.1 4.4 %collective-permute-start.15 = (f32[1,1024]{1,0:T(1,128)S(1)}, f32[1,1024]{1,0:T(1,128)S(1)}, u32[]{:S(2)}, u32[]{:S(2)}) collective-permute-start(f32[1,1024]{1,0:T(1,128)S(1)} %get-tuple-element.18), channel_id=1, source_target_pairs={{0,1},{1,2},{2,3},{4,5},{5,6},{6,7},{8,9},{9,10},{10,11},{12,13},{... | collective-permute-start | bytes 12296 | tf_op jit(solution)/shard_map/ppermute | solution.py:21
  195.6 31.9 %collective-permute-start.16 = (f32[256,1024]{1,0:T(8,128)S(1)}, f32[256,1024]{1,0:T(8,128)S(1)}, u32[]{:S(2)}, u32[]{:S(2)}) collective-permute-start(f32[256,1024]{1,0:T(8,128)S(1)} %fusion.114), channel_id=1, source_target_pairs={{0,4},{4,8},{8,12},{12,16},{16,20},{20,24},{24,28},{28,32},{32,36}... | collective-permute-start | bytes 3145736 | tf_op jit(solution)/shard_map/ppermute | solution.py:30
  228.5 5.6 %collective-permute-start.17 = (f32[1,1024]{1,0:T(1,128)S(1)}, f32[1,1024]{1,0:T(1,128)S(1)}, u32[]{:S(2)}, u32[]{:S(2)}) collective-permute-start(f32[1,1024]{1,0:T(1,128)S(1)} %get-tuple-element.17), channel_id=1, source_target_pairs={{1,0},{2,1},{3,2},{5,4},{6,5},{7,6},{9,8},{10,9},{11,10},{13,12},{... | collective-permute-start | bytes 12296 | tf_op jit(solution)/shard_map/ppermute | solution.py:22
  230.4 4.4 %collective-permute-start.18 = (f32[1,1024]{1,0:T(1,128)S(1)}, f32[1,1024]{1,0:T(1,128)S(1)}, u32[]{:S(2)}, u32[]{:S(2)}) collective-permute-start(f32[1,1024]{1,0:T(1,128)S(1)} %get-tuple-element.16), channel_id=1, source_target_pairs={{0,1},{1,2},{2,3},{4,5},{5,6},{6,7},{8,9},{9,10},{10,11},{12,13},{... | collective-permute-start | bytes 12296 | tf_op jit(solution)/shard_map/ppermute | solution.py:21
  239.7 31.8 %collective-permute-start.19 = (f32[256,1024]{1,0:T(8,128)S(1)}, f32[256,1024]{1,0:T(8,128)S(1)}, u32[]{:S(2)}, u32[]{:S(2)}) collective-permute-start(f32[256,1024]{1,0:T(8,128)S(1)} %fusion.120), channel_id=1, source_target_pairs={{0,4},{4,8},{8,12},{12,16},{16,20},{20,24},{24,28},{28,32},{32,36}... | collective-permute-start | bytes 3145736 | tf_op jit(solution)/shard_map/ppermute | solution.py:30
  271.5 5.6 %collective-permute-start.20 = (f32[1,1024]{1,0:T(1,128)S(1)}, f32[1,1024]{1,0:T(1,128)S(1)}, u32[]{:S(2)}, u32[]{:S(2)}) collective-permute-start(f32[1,1024]{1,0:T(1,128)S(1)} %get-tuple-element.15), channel_id=1, source_target_pairs={{1,0},{2,1},{3,2},{5,4},{6,5},{7,6},{9,8},{10,9},{11,10},{13,12},{... | collective-permute-start | bytes 12296 | tf_op jit(solution)/shard_map/ppermute | solution.py:22
  273.4 4.4 %collective-permute-start.21 = (f32[1,1024]{1,0:T(1,128)S(1)}, f32[1,1024]{1,0:T(1,128)S(1)}, u32[]{:S(2)}, u32[]{:S(2)}) collective-permute-start(f32[1,1024]{1,0:T(1,128)S(1)} %get-tuple-element.14), channel_id=1, source_target_pairs={{0,1},{1,2},{2,3},{4,5},{5,6},{6,7},{8,9},{9,10},{10,11},{12,13},{... | collective-permute-start | bytes 12296 | tf_op jit(solution)/shard_map/ppermute | solution.py:21
  279.2 31.8 %collective-permute-start.22 = (f32[256,1024]{1,0:T(8,128)S(1)}, f32[256,1024]{1,0:T(8,128)S(1)}, u32[]{:S(2)}, u32[]{:S(2)}) collective-permute-start(f32[256,1024]{1,0:T(8,128)S(1)} %fusion.126), channel_id=1, source_target_pairs={{0,4},{4,8},{8,12},{12,16},{16,20},{20,24},{24,28},{28,32},{32,36}... | collective-permute-start | bytes 3145736 | tf_op jit(solution)/shard_map/ppermute | solution.py:30
  311.0 5.6 %collective-permute-start.23 = (f32[1,1024]{1,0:T(1,128)S(1)}, f32[1,1024]{1,0:T(1,128)S(1)}, u32[]{:S(2)}, u32[]{:S(2)}) collective-permute-start(f32[1,1024]{1,0:T(1,128)S(1)} %get-tuple-element.13), channel_id=1, source_target_pairs={{1,0},{2,1},{3,2},{5,4},{6,5},{7,6},{9,8},{10,9},{11,10},{13,12},{... | collective-permute-start | bytes 12296 | tf_op jit(solution)/shard_map/ppermute | solution.py:22
  313.0 4.4 %collective-permute-start.24 = (f32[1,1024]{1,0:T(1,128)S(1)}, f32[1,1024]{1,0:T(1,128)S(1)}, u32[]{:S(2)}, u32[]{:S(2)}) collective-permute-start(f32[1,1024]{1,0:T(1,128)S(1)} %get-tuple-element.12), channel_id=1, source_target_pairs={{0,1},{1,2},{2,3},{4,5},{5,6},{6,7},{8,9},{9,10},{10,11},{12,13},{... | collective-permute-start | bytes 12296 | tf_op jit(solution)/shard_map/ppermute | solution.py:21
  318.8 31.9 %collective-permute-start.25 = (f32[256,1024]{1,0:T(8,128)S(1)}, f32[256,1024]{1,0:T(8,128)S(1)}, u32[]{:S(2)}, u32[]{:S(2)}) collective-permute-start(f32[256,1024]{1,0:T(8,128)S(1)} %fusion.132), channel_id=1, source_target_pairs={{0,4},{4,8},{8,12},{12,16},{16,20},{20,24},{24,28},{28,32},{32,36}... | collective-permute-start | bytes 3145736 | tf_op jit(solution)/shard_map/ppermute | solution.py:30
  350.6 5.6 %collective-permute-start.26 = (f32[1,1024]{1,0:T(1,128)S(1)}, f32[1,1024]{1,0:T(1,128)S(1)}, u32[]{:S(2)}, u32[]{:S(2)}) collective-permute-start(f32[1,1024]{1,0:T(1,128)S(1)} %get-tuple-element.11), channel_id=1, source_target_pairs={{1,0},{2,1},{3,2},{5,4},{6,5},{7,6},{9,8},{10,9},{11,10},{13,12},{... | collective-permute-start | bytes 12296 | tf_op jit(solution)/shard_map/ppermute | solution.py:22
  352.5 4.4 %collective-permute-start.27 = (f32[1,1024]{1,0:T(1,128)S(1)}, f32[1,1024]{1,0:T(1,128)S(1)}, u32[]{:S(2)}, u32[]{:S(2)}) collective-permute-start(f32[1,1024]{1,0:T(1,128)S(1)} %get-tuple-element.10), channel_id=1, source_target_pairs={{0,1},{1,2},{2,3},{4,5},{5,6},{6,7},{8,9},{9,10},{10,11},{12,13},{... | collective-permute-start | bytes 12296 | tf_op jit(solution)/shard_map/ppermute | solution.py:21
  358.3 31.8 %collective-permute-start.28 = (f32[256,1024]{1,0:T(8,128)S(1)}, f32[256,1024]{1,0:T(8,128)S(1)}, u32[]{:S(2)}, u32[]{:S(2)}) collective-permute-start(f32[256,1024]{1,0:T(8,128)S(1)} %fusion.138), channel_id=1, source_target_pairs={{0,4},{4,8},{8,12},{12,16},{16,20},{20,24},{24,28},{28,32},{32,36}... | collective-permute-start | bytes 3145736 | tf_op jit(solution)/shard_map/ppermute | solution.py:30
  390.1 5.6 %collective-permute-start.29 = (f32[1,1024]{1,0:T(1,128)S(1)}, f32[1,1024]{1,0:T(1,128)S(1)}, u32[]{:S(2)}, u32[]{:S(2)}) collective-permute-start(f32[1,1024]{1,0:T(1,128)S(1)} %get-tuple-element.9), channel_id=1, source_target_pairs={{1,0},{2,1},{3,2},{5,4},{6,5},{7,6},{9,8},{10,9},{11,10},{13,12},{... | collective-permute-start | bytes 12296 | tf_op jit(solution)/shard_map/ppermute | solution.py:22
  397.9 6.1 %collective-permute-start.31 = (f32[3,1024]{1,0:T(4,128)S(1)}, f32[3,1024]{1,0:T(4,128)S(1)}, u32[]{:S(2)}, u32[]{:S(2)}) collective-permute-start(f32[3,1024]{1,0:T(4,128)S(1)} %get-tuple-element.6), channel_id=1, source_target_pairs={{0,1},{1,2},{2,3},{4,5},{5,6},{6,7},{8,9},{9,10},{10,11},{12,13},{... | collective-permute-start | bytes 36872 | tf_op jit(solution)/shard_map/ppermute | solution.py:21
  402.1 5.1 %collective-permute-start.32 = (f32[3,1024]{1,0:T(4,128)S(1)}, f32[3,1024]{1,0:T(4,128)S(1)}, u32[]{:S(2)}, u32[]{:S(2)}) collective-permute-start(f32[3,1024]{1,0:T(4,128)S(1)} %get-tuple-element.7), channel_id=1, source_target_pairs={{1,0},{2,1},{3,2},{5,4},{6,5},{7,6},{9,8},{10,9},{11,10},{13,12},{... | collective-permute-start | bytes 36872 | tf_op jit(solution)/shard_map/ppermute | solution.py:22
  (20 other events, 179.6 us)
where the time goes:
time: 413 us; the launch traced here: 412 us
  waiting for transfers between devices  271 us (66%)
  starting transfers between devices  86.8 us (21%)
  other arithmetic  47.6 us (12%)
  local copies, waits for them, and re-layouts  5.19 us (1%)
    ppermute x9, waiting for transfers between devices, from_behind(): lax.ppermute(value, axis, [(source, source + steps) for source in range(i...  261 us
    ppermute x12, starting transfers between devices, extended(): before = lax.ppermute(last, axis, up)  44 us
    ppermute x12, starting transfers between devices, extended(): after = lax.ppermute(initial, axis, down)  23.7 us
    select_n x8, other arithmetic, local(): coarse = jnp.where(active, updated, coarse)  21 us
    ppermute x9, starting transfers between devices, from_behind(): lax.ppermute(value, axis, [(source, source + steps) for source in range(i...  19.1 us
    concatenate x12, other arithmetic, extended(): shard = jnp.concatenate([before, shard, after], axis=dim)  11.5 us
    select_n x8, other arithmetic, deep_step(): return jnp.where(inside, stepped, jnp.zeros_like(stepped))  9.82 us
  transfers between devices with their start and end apart: 33, of which 19 were waited for; matrix products, arithmetic and copies ran while one was open for 1% of the time, Pallas kernels for 0%

commit v1 on v0

v1 whole, which is shorter than its diff:
```python
import functools

import jax
import jax.numpy as jnp
from jax import lax
from jax.experimental import pallas as pl
from jax.experimental.pallas import tpu as pltpu
from jax.sharding import PartitionSpec as P

STEPS = 4
GROUP = 4
DIFFUSION = 0.05
RING = 8
HALO = 24
LANES = 128
FRAME = 16
EDGE = 11
PACK = 64
TAIL = 4
GUARD = 8


def lane_index():
    return lax.broadcasted_iota(jnp.int32, (8, LANES), 1)


def neighbour_sum(tiles, up, down):
    lane = lane_index()
    count = len(tiles)
    right_turned = [pltpu.roll(t, 1, 1) for t in tiles]
    left_turned = [pltpu.roll(t, LANES - 1, 1) for t in tiles]
    sums = []
    for i in range(count):
        left = jnp.where(lane == 0, right_turned[i - 1], right_turned[i])
        right = jnp.where(lane == LANES - 1, left_turned[(i + 1) % count], left_turned[i])
        sums.append((up[i] + down[i]) + (left + right))
    return sums


def stepped(ref, at, row, coefs):
    count = len(coefs)
    tiles = [ref[at + (i, pl.ds(row, 8), slice(None))] for i in range(count)]
    up = [ref[at + (i, pl.ds(row - 1, 8), slice(None))] for i in range(count)]
    down = [ref[at + (i, pl.ds(row + 1, 8), slice(None))] for i in range(count)]
    sums = neighbour_sum(tiles, up, down)
    out = [k * s + c * (m - r * (c * c)) for c, s, (k, r, m) in zip(tiles, sums, coefs)]
    return out, tiles


def rows_of(ref, kinds, count, row):
    return [tuple(ref[k, i, pl.ds(row, 8), :] for k in kinds) for i in range(count)]


def each_block(first, last, body, unroll=1):
    def trip(i, carry):
        body(pl.multiple_of(first + 8 * i, 8))
        return carry

    lax.fori_loop(0, (last - first) // 8, trip, 0, unroll=unroll)


def relax_kernel(g_ref, k_ref, r_ref, lo_ref, hi_ref, packed_ref, own_ref, u_ref, w_ref, c_ref):
    rows, columns = g_ref.shape
    tiles = columns // LANES
    ext = rows + 2 * HALO
    top = GUARD + HALO
    zero8 = jnp.zeros((GUARD, LANES), jnp.float32)

    def fill(put, body_ref, part):
        for t in range(tiles):
            cols = slice(t * LANES, (t + 1) * LANES)
            put(t, GUARD, HALO, lambda a, n: lo_ref[part, pl.ds(a, n), cols])
            put(t, top, rows, lambda a, n: body_ref[pl.ds(a, n), cols])
            put(t, top + rows, HALO, lambda a, n: hi_ref[part, pl.ds(a, n), cols])

    def put_u(t, at, n, load):
        u_ref[t, at : at + n, :] = load(0, n)

    def put_k(t, at, n, load):
        c_ref[0, t, at : at + n, :] = DIFFUSION * load(0, n)

    def put_r(t, at, n, load):
        rate = load(0, n)
        c_ref[1, t, at : at + n, :] = rate
        c_ref[2, t, at : at + n, :] = 1.0 - 4.0 * c_ref[0, t, at : at + n, :] + rate

    fill(put_u, g_ref, 0)
    fill(put_k, k_ref, 1)
    fill(put_r, r_ref, 2)
    pad = jnp.zeros((ext + 2 * GUARD, LANES), jnp.float32)
    u_ref[tiles] = pad
    w_ref[tiles] = pad
    for kind in range(2):
        c_ref[kind, tiles] = pad
    c_ref[2, tiles] = pad + 1.0
    for t in range(tiles):
        for ref in (u_ref, w_ref):
            ref[t, 0:GUARD, :] = zero8
            ref[t, GUARD + ext : ext + 2 * GUARD, :] = zero8

    def march(src, dst, first, last):
        def body(row):
            out, _ = stepped(src, (), row, rows_of(c_ref, (0, 1, 2), tiles + 1, row))
            for t in range(tiles):
                dst[t, pl.ds(row, 8), :] = out[t]

        each_block(first, last, body)

    march(u_ref, w_ref, GUARD, GUARD + ext)
    march(w_ref, u_ref, GUARD, GUARD + ext)
    march(u_ref, w_ref, GUARD + 8, GUARD + ext - 8)
    march(w_ref, u_ref, GUARD + 8, GUARD + ext - 8)

    frame = rows + 2 * FRAME
    base = top - FRAME
    lane = lane_index()
    for c in range(RING):
        packed_ref[c, 0:frame, :] = u_ref[c, base : base + frame, :]
        after, before = c + 1, (c - 1) % (tiles + 1)
        for block in range(PACK // 8):
            acc = jnp.zeros((8, LANES), jnp.float32)
            for part in range(pl.cdiv(frame, PACK)):
                at = part * PACK + block * 8
                if at < frame:
                    edge = jnp.where(
                        lane < LANES // 2,
                        u_ref[after, base + at : base + at + 8, :],
                        u_ref[before, base + at : base + at + 8, :],
                    )
                    begin = 2 * EDGE * part
                    turned = pltpu.roll(edge, EDGE + begin, 1)
                    acc = jnp.where((lane >= begin) & (lane < begin + 2 * EDGE), turned, acc)
            packed_ref[c, frame + 8 * block : frame + 8 * block + 8, :] = acc

    mine = (lax.axis_index("tm") + 1) % RING
    after, before = mine + 1, lax.rem(mine + tiles, tiles + 1)
    near = (lane < EDGE) | (lane >= LANES - EDGE)
    for kind in range(3):
        own_ref[kind, 0, 0:GUARD, :] = zero8
        own_ref[kind, 1, 0:GUARD, :] = zero8
        own_ref[kind, 0, GUARD + frame :, :] = zero8
        own_ref[kind, 1, GUARD + frame :, :] = zero8

        def body(row, kind=kind):
            src = row + base - GUARD
            own_ref[kind, 0, pl.ds(row, 8), :] = c_ref[kind, mine, pl.ds(src, 8), :]
            edge = jnp.where(
                lane < LANES // 2,
                c_ref[kind, after, pl.ds(src, 8), :],
                c_ref[kind, before, pl.ds(src, 8), :],
            )
            far = 1.0 if kind == 2 else 0.0
            own_ref[kind, 1, pl.ds(row, 8), :] = jnp.where(near, edge, far)

        each_block(GUARD, GUARD + frame, body)


def unpack(src_ref, at, dst_ref, to, frame):
    zero8 = jnp.zeros((GUARD, LANES), jnp.float32)
    for i in range(2):
        dst_ref[to, i, 0:GUARD, :] = zero8
        dst_ref[to, i, GUARD + frame : frame + 2 * GUARD, :] = zero8
    dst_ref[to, 0, GUARD : GUARD + frame, :] = src_ref[at + (slice(0, frame),)]
    for part in range(pl.cdiv(frame, PACK)):
        count = min(PACK, frame - part * PACK)
        block = src_ref[at + (slice(frame, frame + count),)]
        turned = pltpu.roll(block, (-(2 * EDGE * part + EDGE)) % LANES, 1)
        dst_ref[to, 1, GUARD + part * PACK : GUARD + part * PACK + count, :] = turned


def pack(src_ref, at, dst_ref, frame):
    lane = lane_index()
    dst_ref[0:frame, :] = src_ref[at, 0, GUARD : GUARD + frame, :]
    for block in range(PACK // 8):
        acc = jnp.zeros((8, LANES), jnp.float32)
        for part in range(pl.cdiv(frame, PACK)):
            row = part * PACK + block * 8
            if row < frame:
                begin = 2 * EDGE * part
                edge = src_ref[at, 1, GUARD + row : GUARD + row + 8, :]
                turned = pltpu.roll(edge, EDGE + begin, 1)
                acc = jnp.where((lane >= begin) & (lane < begin + 2 * EDGE), turned, acc)
        dst_ref[frame + 8 * block : frame + 8 * block + 8, :] = acc


def coarse_coefs(own_ref, row):
    fine = rows_of(own_ref, (0, 1, 2), 2, row)
    return [(STEPS * k, STEPS * r, STEPS * m - (STEPS - 1.0)) for k, r, m in fine]


def defects(in_ref, first, own_ref, x_ref, y_ref, d_ref, frame):
    for f in range(GROUP):
        unpack(in_ref, (first + f,), x_ref, f, frame)
        zero8 = jnp.zeros((GUARD, LANES), jnp.float32)
        for i in range(2):
            y_ref[f, i, 0:GUARD, :] = zero8
            y_ref[f, i, GUARD + frame : frame + 2 * GUARD, :] = zero8
    for step in range(STEPS):
        src, dst = (x_ref, y_ref) if step % 2 == 0 else (y_ref, x_ref)

        def body(row, step=step, src=src, dst=dst):
            coefs = rows_of(own_ref, (0, 1, 2), 2, row)
            for f in range(GROUP):
                out, old = stepped(src, (f,), row, coefs)
                for i in range(2):
                    dst[f, i, pl.ds(row, 8), :] = out[i]
                    if step == 0:
                        d_ref[f, i, pl.ds(row, 8), :] = STEPS * out[i] - (STEPS - 1.0) * old[i]
                    if step == STEPS - 1:
                        d_ref[f, i, pl.ds(row, 8), :] = out[i] - d_ref[f, i, pl.ds(row, 8), :]

        each_block(GUARD, GUARD + frame, body)


def chain_step(src_ref, at, dst_ref, to, own_ref, d_ref, which, frame, also=None):
    def body(row):
        out, _ = stepped(src_ref, (at,), row, coarse_coefs(own_ref, row))
        for i in range(2):
            value = out[i] + d_ref[which, i, pl.ds(row, 8), :]
            dst_ref[to, i, pl.ds(row, 8), :] = value

    each_block(GUARD, GUARD + frame, body)


def later_kernel(in_ref, own_ref, d_ref, sent_ref, x_ref, y_ref):
    frame = in_ref.shape[1] - PACK
    defects(in_ref, GROUP, own_ref, x_ref, y_ref, d_ref, frame)
    chain_step(x_ref, 0, y_ref, 0, own_ref, d_ref, 1, frame)
    chain_step(y_ref, 0, x_ref, 0, own_ref, d_ref, 2, frame)
    chain_step(x_ref, 0, y_ref, 0, own_ref, d_ref, 3, frame)
    pack(y_ref, 0, sent_ref, frame)


def emit(src_ref, at, out_ref, field, strip):
    z = lax.axis_index("tm") % RING
    slot = (field + 1 - z + RING) % RING
    begin = GUARD + FRAME - TAIL
    out_ref[slot] = src_ref[at, 0, begin : begin + strip + 2 * TAIL, :]


def earlier_kernel(in_ref, own_ref, later_d_ref, d_ref, one_ref, out_ref, x_ref, y_ref):
    frame = in_ref.shape[1] - PACK
    strip = frame - 2 * FRAME
    defects(in_ref, 0, own_ref, x_ref, y_ref, d_ref, frame)
    unpack(in_ref, (1,), one_ref, 0, frame)

    @pl.when(lax.axis_index("tm") + 1 < RING)
    def _():
        x_ref[0] = one_ref[0]

    @pl.when(lax.axis_index("tm") == lax.axis_size("tm") - 1)
    def _():
        x_ref[0] = one_ref[0]

    chain_step(x_ref, 0, y_ref, 0, own_ref, d_ref, 1, frame)
    chain_step(y_ref, 0, x_ref, 0, own_ref, d_ref, 2, frame)
    chain_step(x_ref, 0, y_ref, 0, own_ref, d_ref, 3, frame)
    for i in range(GROUP):
        src, dst = (y_ref, x_ref) if i % 2 == 0 else (x_ref, y_ref)
        chain_step(src, 0, dst, 0, own_ref, later_d_ref, i, frame)
        emit(dst, 0, out_ref, GROUP + i, strip)


def last_kernel(got_ref, own_ref, d_ref, one_ref, half_ref, out_ref, x_ref, y_ref):
    frame = got_ref.shape[0] - PACK
    strip = frame - 2 * FRAME
    out_ref[...] = half_ref[...]
    unpack(got_ref, (), x_ref, 0, frame)
    zero8 = jnp.zeros((GUARD, LANES), jnp.float32)
    for i in range(2):
        y_ref[0, i, 0:GUARD, :] = zero8
        y_ref[0, i, GUARD + frame : frame + 2 * GUARD, :] = zero8
    for i in range(GROUP):
        src, dst = (x_ref, y_ref) if i % 2 == 0 else (y_ref, x_ref)
        chain_step(src, 0, dst, 0, own_ref, d_ref, i, frame)
        if i == 0:
            member = (lax.axis_index("tm") + 1) % lax.axis_size("tm")

            @pl.when(member < RING)
            def _():
                dst[0] = one_ref[0]

        emit(dst, 0, out_ref, i, strip)


def fine_kernel(g_ref, k_ref, r_ref, lo_ref, hi_ref, *refs):
    blocks, (points_ref, last_ref, u_ref, w_ref, c_ref) = refs[:RING], refs[RING:]
    rows, columns = g_ref.shape
    tiles = columns // LANES
    tall = rows + 2 * TAIL
    zero8 = jnp.zeros((GUARD, LANES), jnp.float32)
    me = lax.axis_index("tm")
    for ref in (u_ref, w_ref):
        ref[tiles] = jnp.zeros((tall + 2 * GUARD, LANES), jnp.float32)
        for t in range(tiles):
            ref[t, 0:GUARD, :] = zero8
            ref[t, GUARD + tall : tall + 2 * GUARD, :] = zero8
    inner = GUARD + TAIL

    def spread(part, body_ref, store):
        for t in range(tiles):
            cols = slice(t * LANES, (t + 1) * LANES)
            store(t, GUARD, TAIL, lo_ref[part, HALO - TAIL : HALO, cols])
            store(t, inner, rows, body_ref[:, cols])
            store(t, inner + rows, TAIL, hi_ref[part, 0:TAIL, cols])

    def store_k(t, at, n, value):
        c_ref[0, t, at : at + n, :] = DIFFUSION * value

    def store_r(t, at, n, value):
        c_ref[1, t, at : at + n, :] = value
        c_ref[2, t, at : at + n, :] = 1.0 - 4.0 * c_ref[0, t, at : at + n, :] + value

    def store_u(t, at, n, value):
        u_ref[t, at : at + n, :] = value

    spread(1, k_ref, store_k)
    spread(2, r_ref, store_r)
    pad = jnp.zeros((tall + 2 * GUARD, LANES), jnp.float32)
    c_ref[0, tiles] = pad
    c_ref[1, tiles] = pad
    c_ref[2, tiles] = pad + 1.0

    @pl.when(me == 0)
    def _():
        spread(0, g_ref, store_u)

    @pl.when(me > 0)
    def _():
        for distance in range(RING):
            chunk = (me - distance + 1 + RING) % RING
            u_ref[chunk, GUARD : GUARD + tall, :] = blocks[distance][...]

    for t in range(tiles):
        points_ref[:, t * LANES : (t + 1) * LANES] = u_ref[t, inner : inner + rows, :]
    for step in range(STEPS - 1):
        src, dst = (u_ref, w_ref) if step % 2 == 0 else (w_ref, u_ref)

        def body(row, src=src, dst=dst):
            out, _ = stepped(src, (), row, rows_of(c_ref, (0, 1, 2), tiles + 1, row))
            for t in range(tiles):
                dst[t, pl.ds(row, 8), :] = out[t]

        each_block(GUARD, GUARD + tall, body)
    for t in range(tiles):
        last_ref[:, t * LANES : (t + 1) * LANES] = w_ref[t, inner : inner + rows, :]


def call(kernel, outs, scratch, cost, *args):
    flops, moved = cost
    vmem = pl.BlockSpec(memory_space=pltpu.VMEM)
    return pl.pallas_call(
        kernel,
        out_shape=[jax.ShapeDtypeStruct(s, jnp.float32) for s in outs],
        in_specs=[vmem] * len(args),
        out_specs=[vmem] * len(outs),
        scratch_shapes=[pltpu.VMEM(s, jnp.float32) for s in scratch],
        cost_estimate=pl.CostEstimate(flops=flops, bytes_accessed=moved, transcendentals=0),
        compiler_params=pltpu.CompilerParams(vmem_limit_bytes=56 << 20),
    )(*args)


def local(guess, kappa, rate):
    intervals, strips = lax.axis_size("tm"), lax.axis_size("space")
    state = guess[0]
    rows, columns = state.shape
    tiles = columns // LANES
    edges = jnp.stack([state, kappa, rate])
    up = [(i, i + 1) for i in range(strips - 1)]
    down = [(i + 1, i) for i in range(strips - 1)]
    lo = lax.ppermute(edges[:, rows - HALO :], "space", up)
    hi = lax.ppermute(edges[:, :HALO], "space", down)

    frame = rows + 2 * FRAME
    ext = rows + 2 * HALO + 2 * GUARD
    wide = frame + 2 * GUARD
    packed, own = call(
        relax_kernel,
        [(RING, frame + PACK, LANES), (3, 2, wide, LANES)],
        [(tiles + 1, ext, LANES), (tiles + 1, ext, LANES), (3, tiles + 1, ext, LANES)],
        (40 * rows * columns, 16 * rows * columns),
        state, kappa, rate, lo, hi,
    )
    rings = [[(RING * m + i - 1) % intervals for i in range(RING)] for m in range(intervals // RING)]
    fields = lax.all_to_all(packed, "tm", 0, 0, axis_index_groups=rings, tiled=True)
    four = (GROUP, 2, wide, LANES)
    later_d, sent = call(
        later_kernel, [four, (frame + PACK, LANES)], [four, four],
        (20 * rows * columns, 8 * rows * columns), fields, own,
    )
    got = lax.ppermute(sent, "tm", [(i, i + RING) for i in range(intervals - RING)]
                       + [(intervals - RING + i, i) for i in range(RING)])
    tall = rows + 2 * TAIL
    d, one, half = call(
        earlier_kernel, [four, (1, 2, wide, LANES), (RING, tall, LANES)], [four, four],
        (20 * rows * columns, 8 * rows * columns), fields, own, later_d,
    )
    (out,) = call(
        last_kernel, [(RING, tall, LANES)], [(1, 2, wide, LANES)] * 2,
        (4 * rows * columns, 4 * rows * columns), got, own, d, one, half,
    )
    blocks = []
    for distance in range(RING):
        pairs = []
        for m in range(intervals // RING):
            for i in range(RING):
                source = (RING * m + i - 1) % intervals
                field = (source + distance - 1) % RING
                pairs.append((source, (RING * m + 1 + field) % intervals))
        blocks.append(lax.ppermute(out[distance], "tm", pairs))
    c_points, last_fine = call(
        fine_kernel, [(rows, columns)] * 2,
        [(tiles + 1, tall + 2 * GUARD, LANES)] * 2 + [(3, tiles + 1, tall + 2 * GUARD, LANES)],
        (30 * rows * columns, 16 * rows * columns),
        state, kappa, rate, lo, hi, *blocks,
    )
    return c_points[None], last_fine[None]


def solution(mesh):
    return jax.shard_map(
        local,
        mesh=mesh,
        in_specs=(P("tm", "space", None), P("space", None), P("space", None)),
        out_specs=(P("tm", "space", None), P("tm", "space", None)),
        check_vma=False,
    )
```

time: 413 us -> 209 us (0.51)
  waiting for transfers between devices: 271 us -> 32.2 us
  Pallas kernels: 0 us -> 107 us
  starting transfers between devices: 86.8 us -> 15.5 us
  other arithmetic: 47.6 us -> 1.17 us
  blocking collectives: 0 us -> 45.7 us
    ppermute x33 -> x11, waiting for transfers between devices: 271 us -> 32.2 us  [the longest x8 28.6 us: local(): blocks.append(lax.ppermute(out[distance], 'tm', pairs))]
    pallas_call x0 -> x5, Pallas kernels: none -> 107 us  [call(): pl.pallas_call(kernel, out_shape=[jax.ShapeDtypeStruct(s, jnp.float32) fo...]
    ppermute x33 -> x11, starting transfers between devices: 86.8 us -> 15.5 us  [the longest x8 9.94 us: local(): blocks.append(lax.ppermute(out[distance], 'tm', pairs))]
    all_to_all x0 -> x1, blocking collectives: none -> 45.7 us  [local(): lax.all_to_all(packed, 'tm', 0, 0, axis_index_groups=rings, tiled=True)]
    select_n x17 -> x0, other arithmetic: 33 us -> none  [the longest x8 21 us: local(): coarse = jnp.where(active, updated, coarse)]
    concatenate x12 -> x0, other arithmetic: 11.5 us -> none  [extended(): shard = jnp.concatenate([before, shard, after], axis=dim)]
  transfers between devices with their start and end apart: 33 -> 11, of which waited for: 19 -> 7; matrix products, arithmetic and copies ran while one was open for 1% -> 0% of each run, Pallas kernels for 0% -> 18%
where the time goes in v1:
time: 209 us; the launch traced here: 207 us
  Pallas kernels  107 us (51%)
  blocking collectives  45.7 us (22%)
  waiting for transfers between devices  32.2 us (15%)
  starting transfers between devices  15.5 us (7%)
  local copies, waits for them, and re-layouts  4.04 us (2%)
    pallas_call x5, Pallas kernels, call(): pl.pallas_call(kernel, out_shape=[jax.ShapeDtypeStruct(s, jnp.float32) fo...  107 us
    all_to_all x1, blocking collectives, local(): lax.all_to_all(packed, 'tm', 0, 0, axis_index_groups=rings, tiled=True)  45.7 us
    ppermute x8, waiting for transfers between devices, local(): blocks.append(lax.ppermute(out[distance], 'tm', pairs))  28.6 us
    ppermute x8, starting transfers between devices, local(): blocks.append(lax.ppermute(out[distance], 'tm', pairs))  9.94 us
  transfers between devices with their start and end apart: 11, of which 7 were waited for; matrix products, arithmetic and copies ran while one was open for 0% of the time, Pallas kernels for 18%

profile of v1, /device:TPU:17, one launch (start us, length us, event | category | flops | bytes accessed | tf_op | source)
XLA Modules:
  0.0 206.7 jit_solution(3373513629335934175)
XLA Ops:
  0.6 1.2 pad_maximum_fusion
  1.8 2.6 %collective-permute-start.1 = (f32[3,24,1024]{2,1,0:T(8,128)S(1)}, f32[3,24,1024]{2,1,0:T(8,128)S(1)}, u32[]{:S(2)}, u32[]{:S(2)}) collective-permute-start(f32[3,24,1024]{2,1,0:T(8,128)S(1)} %get-tuple-element.20), channel_id=1, source_target_pairs={{1,0},{2,1},{3,2},{5,4},{6,5},{7,6},{9,8},{10,9},{11,10},{13,12},{... | collective-permute-start | bytes 884744 | tf_op jit(solution)/shard_map/ppermute | solution.py:372
  4.4 3.0 %collective-permute-start = (f32[3,24,1024]{2,1,0:T(8,128)S(1)}, f32[3,24,1024]{2,1,0:T(8,128)S(1)}, u32[]{:S(2)}, u32[]{:S(2)}) collective-permute-start(f32[3,24,1024]{2,1,0:T(8,128)S(1)} %get-tuple-element.21), channel_id=1, source_target_pairs={{0,1},{1,2},{2,3},{4,5},{5,6},{6,7},{8,9},{9,10},{10,11},{12,13},{... | collective-permute-start | bytes 884744 | tf_op jit(solution)/shard_map/ppermute | solution.py:371
  7.4 2.5 %collective-permute-done.1.hi_ref = f32[3,24,1024]{2,1,0:T(8,128)S(1)} collective-permute-done((f32[3,24,1024]{2,1,0:T(8,128)S(1)}, f32[3,24,1024]{2,1,0:T(8,128)S(1)}, u32[]{:S(2)}, u32[]{:S(2)}) %collective-permute-start.1) | collective-permute-done | bytes 294944 | tf_op jit(solution)/shard_map/ppermute | solution.py:372
  9.8 1.2 collective-permute-done.lo_ref
  11.0 0.7 copy-done.1
  11.8 19.0 %shard_map.50 = (f32[8,352,128]{2,1,0:T(8,128)}, f32[3,2,304,128]{3,2,1,0:T(8,128)}) custom-call(f32[256,1024]{1,0:T(8,128)} %bitcast.21, f32[256,1024]{1,0:T(8,128)} %k_ref.3, f32[256,1024]{1,0:T(8,128)} %r_ref.3, f32[3,24,1024]{2,1,0:T(8,128)} %copy-done.1, f32[3,24,1024]{2,1,0:T(8,128)} %copy-done), custom_call_target="tpu_custom_call" | custom-call | flops 10485760 | bytes 4194304 | tf_op jit(solution)/shard_map/pallas_call | solution.py:352
  30.7 45.7 %all_to_all.5.in_ref = f32[8,352,128]{2,1,0:T(8,128)} all-to-all(f32[8,352,128]{2,1,0:T(8,128)} %get-tuple-element.11), channel_id=1, replica_groups={{252,0,4,8,12,16,20,24},{28,32,36,40,44,48,52,56},{60,64,68,72,76,80,84..., dimensions={0} | all-to-all | bytes 2883584 | tf_op jit(solution)/shard_map/all_to_all | solution.py:385
  76.4 24.3 %shard_map.51 = (f32[4,2,304,128]{3,2,1,0:T(8,128)}, f32[352,128]{1,0:T(8,128)}) custom-call(f32[8,352,128]{2,1,0:T(8,128)} %all_to_all.5.in_ref, f32[3,2,304,128]{3,2,1,0:T(8,128)} %get-tuple-element.12.own_ref), custom_call_target="tpu_custom_call" | custom-call | flops 5242880 | bytes 2097152 | tf_op jit(solution)/shard_map/pallas_call | solution.py:352
  100.7 0.0 collective-permute-start.2
  100.7 36.3 %shard_map.52 = (f32[4,2,304,128]{3,2,1,0:T(8,128)}, f32[1,2,304,128]{3,2,1,0:T(8,128)}, f32[8,264,128]{2,1,0:T(8,128)}) custom-call(f32[8,352,128]{2,1,0:T(8,128)} %all_to_all.5.in_ref, f32[3,2,304,128]{3,2,1,0:T(8,128)} %get-tuple-element.12.own_ref, f32[4,2,304,128]{3,2,1,0:T(8,128)} %get-tuple-element.14.later_d_ref), custom_call_target="tpu_custom_call" | custom-call | flops 5242880 | bytes 2097152 | tf_op jit(solution)/shard_map/pallas_call | solution.py:352
  137.1 0.0 collective-permute-done.2.got_ref
  137.1 0.7 copy-done.2
  137.7 14.4 %shard_map.53 = f32[8,264,128]{2,1,0:T(8,128)} custom-call(f32[352,128]{1,0:T(8,128)} %copy-done.2, f32[3,2,304,128]{3,2,1,0:T(8,128)} %get-tuple-element.12.own_ref, f32[4,2,304,128]{3,2,1,0:T(8,128)} %get-tuple-element.15.d_ref, f32[1,2,304,128]{3,2,1,0:T(8,128)} %get-tuple-element.16.one_ref, f32[8,264,128]{2,1,0:T(8,128)} %get-tuple-element.17.half_ref), custom_call_target="tpu_custom_call" | custom-call | flops 1048576 | bytes 1048576 | tf_op jit(solution)/shard_map/pallas_call | solution.py:352
  152.1 1.4 slice_bitcast_fusion
  153.5 0.9 collective-permute-start.10
  154.4 1.9 collective-permute-start.9
  156.2 1.4 collective-permute-start.8
  157.6 2.8 %collective-permute-start.7 = (f32[264,128]{1,0:T(8,128)S(1)}, f32[264,128]{1,0:T(8,128)S(1)}, u32[]{:S(2)}, u32[]{:S(2)}) collective-permute-start(f32[264,128]{1,0:T(8,128)S(1)} %get-tuple-element.25), channel_id=1, source_target_pairs={{252,12},{0,16},{4,20},{8,24},{12,28},{16,32},{20,4},{24,8},{28,44... | collective-permute-start | bytes 405512 | tf_op jit(solution)/shard_map/ppermute | solution.py:410
  160.4 0.0 collective-permute-start.6
  160.4 1.6 collective-permute-done.10.refs_7_
  161.9 1.1 collective-permute-start.5
  163.1 8.6 %collective-permute-done.9.refs_6_ = f32[264,128]{1,0:T(8,128)S(1)} collective-permute-done((f32[264,128]{1,0:T(8,128)S(1)}, f32[264,128]{1,0:T(8,128)S(1)}, u32[]{:S(2)}, u32[]{:S(2)}) %collective-permute-start.9) | collective-permute-done | bytes 135200 | tf_op jit(solution)/shard_map/ppermute | solution.py:410
  171.6 0.0 collective-permute-start.4
  171.6 5.6 %collective-permute-done.8.refs_5_ = f32[264,128]{1,0:T(8,128)S(1)} collective-permute-done((f32[264,128]{1,0:T(8,128)S(1)}, f32[264,128]{1,0:T(8,128)S(1)}, u32[]{:S(2)}, u32[]{:S(2)}) %collective-permute-start.8) | collective-permute-done | bytes 135200 | tf_op jit(solution)/shard_map/ppermute | solution.py:410
  177.2 1.9 collective-permute-start.3
  179.2 6.8 %collective-permute-done.6.refs_3_ = f32[264,128]{1,0:T(8,128)S(1)} collective-permute-done((f32[264,128]{1,0:T(8,128)S(1)}, f32[264,128]{1,0:T(8,128)S(1)}, u32[]{:S(2)}, u32[]{:S(2)}) %collective-permute-start.6) | collective-permute-done | bytes 135200 | tf_op jit(solution)/shard_map/ppermute | solution.py:410
  186.0 6.0 %collective-permute-done.4.refs_1_ = f32[264,128]{1,0:T(8,128)S(1)} collective-permute-done((f32[264,128]{1,0:T(8,128)S(1)}, f32[264,128]{1,0:T(8,128)S(1)}, u32[]{:S(2)}, u32[]{:S(2)}) %collective-permute-start.4) | collective-permute-done | bytes 135200 | tf_op jit(solution)/shard_map/ppermute | solution.py:410
  192.0 0.0 collective-permute-done.3.refs_0_
  192.1 0.6 copy-done.9
  192.7 0.7 copy-done.10
  193.3 13.4 %shard_map.54 = (f32[256,1024]{1,0:T(8,128)}, f32[256,1024]{1,0:T(8,128)}) custom-call(f32[256,1024]{1,0:T(8,128)} %bitcast.22, f32[256,1024]{1,0:T(8,128)} %k_ref.3, f32[256,1024]{1,0:T(8,128)} %r_ref.3, f32[3,24,1024]{2,1,0:T(8,128)} %copy-done.1, f32[3,24,1024]{2,1,0:T(8,128)} %copy-done, f32[264,128]{1,0:T(8,128)} %copy-done.10, f32[264,128]{1,0:T(8,128)} %copy-done.9, ...), custom_call_target="tpu_custom_call" | custom-call | flops 7864320 | bytes 4194304 | tf_op jit(solution)/shard_map/pallas_call | solution.py:352
  (20 shorter events, 0.0 us)
Async XLA Ops:
  1.8 8.0 %collective-permute-start.1 = (f32[3,24,1024]{2,1,0:T(8,128)S(1)}, f32[3,24,1024]{2,1,0:T(8,128)S(1)}, u32[]{:S(2)}, u32[]{:S(2)}) collective-permute-start(f32[3,24,1024]{2,1,0:T(8,128)S(1)} %get-tuple-element.20), channel_id=1, source_target_pairs={{1,0},{2,1},{3,2},{5,4},{6,5},{7,6},{9,8},{10,9},{11,10},{13,12},{... | collective-permute-start | bytes 884744 | tf_op jit(solution)/shard_map/ppermute | solution.py:372
  4.4 6.6 %collective-permute-start = (f32[3,24,1024]{2,1,0:T(8,128)S(1)}, f32[3,24,1024]{2,1,0:T(8,128)S(1)}, u32[]{:S(2)}, u32[]{:S(2)}) collective-permute-start(f32[3,24,1024]{2,1,0:T(8,128)S(1)} %get-tuple-element.21), channel_id=1, source_target_pairs={{0,1},{1,2},{2,3},{4,5},{5,6},{6,7},{8,9},{9,10},{10,11},{12,13},{... | collective-permute-start | bytes 884744 | tf_op jit(solution)/shard_map/ppermute | solution.py:371
  9.8 1.2 copy-start
  11.0 0.7 copy-start.1
  100.7 36.3 %collective-permute-start.2 = (f32[352,128]{1,0:T(8,128)}, f32[352,128]{1,0:T(8,128)S(1)}, u32[]{:S(2)}, u32[]{:S(2)}) collective-permute-start(f32[352,128]{1,0:T(8,128)} %get-tuple-element.13), channel_id=1, source_target_pairs={{0,32},{4,36},{8,40},{12,44},{16,48},{20,52},{24,56},{28,60},{32,6... | collective-permute-start | bytes 540680 | tf_op jit(solution)/shard_map/ppermute | solution.py:391
  137.1 0.7 copy-start.2
  153.5 8.5 %collective-permute-start.10 = (f32[264,128]{1,0:T(8,128)S(1)}, f32[264,128]{1,0:T(8,128)S(1)}, u32[]{:S(2)}, u32[]{:S(2)}) collective-permute-start(f32[264,128]{1,0:T(8,128)S(1)} %get-tuple-element.22), channel_id=1, source_target_pairs={{252,24},{0,28},{4,32},{8,4},{12,8},{16,12},{20,16},{24,20},{28,56... | collective-permute-start | bytes 405512 | tf_op jit(solution)/shard_map/ppermute | solution.py:410
  154.4 17.3 %collective-permute-start.9 = (f32[264,128]{1,0:T(8,128)S(1)}, f32[264,128]{1,0:T(8,128)S(1)}, u32[]{:S(2)}, u32[]{:S(2)}) collective-permute-start(f32[264,128]{1,0:T(8,128)S(1)} %get-tuple-element.23), channel_id=1, source_target_pairs={{252,20},{0,24},{4,28},{8,32},{12,4},{16,8},{20,12},{24,16},{28,52... | collective-permute-start | bytes 405512 | tf_op jit(solution)/shard_map/ppermute | solution.py:410
  156.2 21.0 %collective-permute-start.8 = (f32[264,128]{1,0:T(8,128)S(1)}, f32[264,128]{1,0:T(8,128)S(1)}, u32[]{:S(2)}, u32[]{:S(2)}) collective-permute-start(f32[264,128]{1,0:T(8,128)S(1)} %get-tuple-element.24), channel_id=1, source_target_pairs={{252,16},{0,20},{4,24},{8,28},{12,32},{16,4},{20,8},{24,12},{28,48... | collective-permute-start | bytes 405512 | tf_op jit(solution)/shard_map/ppermute | solution.py:410
  157.6 21.6 %collective-permute-start.7 = (f32[264,128]{1,0:T(8,128)S(1)}, f32[264,128]{1,0:T(8,128)S(1)}, u32[]{:S(2)}, u32[]{:S(2)}) collective-permute-start(f32[264,128]{1,0:T(8,128)S(1)} %get-tuple-element.25), channel_id=1, source_target_pairs={{252,12},{0,16},{4,20},{8,24},{12,28},{16,32},{20,4},{24,8},{28,44... | collective-permute-start | bytes 405512 | tf_op jit(solution)/shard_map/ppermute | solution.py:410
  160.4 25.6 %collective-permute-start.6 = (f32[264,128]{1,0:T(8,128)S(1)}, f32[264,128]{1,0:T(8,128)S(1)}, u32[]{:S(2)}, u32[]{:S(2)}) collective-permute-start(f32[264,128]{1,0:T(8,128)S(1)} %get-tuple-element.26), channel_id=1, source_target_pairs={{252,8},{0,12},{4,16},{8,20},{12,24},{16,28},{20,32},{24,4},{28,40... | collective-permute-start | bytes 405512 | tf_op jit(solution)/shard_map/ppermute | solution.py:410
  161.9 30.1 %copy-start.3 = (f32[264,128]{1,0:T(8,128)}, f32[264,128]{1,0:T(8,128)S(1)}, u32[]{:S(2)}) copy-start(f32[264,128]{1,0:T(8,128)S(1)} %collective-permute-done.10.refs_7_) | copy-start | bytes 405508
  161.9 24.0 %collective-permute-start.5 = (f32[264,128]{1,0:T(8,128)S(1)}, f32[264,128]{1,0:T(8,128)S(1)}, u32[]{:S(2)}, u32[]{:S(2)}) collective-permute-start(f32[264,128]{1,0:T(8,128)S(1)} %get-tuple-element.27), channel_id=1, source_target_pairs={{252,4},{0,8},{4,12},{8,16},{12,20},{16,24},{20,28},{24,32},{28,36... | collective-permute-start | bytes 405512 | tf_op jit(solution)/shard_map/ppermute | solution.py:410
  171.6 20.4 %copy-start.4 = (f32[264,128]{1,0:T(8,128)}, f32[264,128]{1,0:T(8,128)S(1)}, u32[]{:S(2)}) copy-start(f32[264,128]{1,0:T(8,128)S(1)} %collective-permute-done.9.refs_6_) | copy-start | bytes 405508
  171.6 20.4 %collective-permute-start.4 = (f32[264,128]{1,0:T(8,128)S(1)}, f32[264,128]{1,0:T(8,128)S(1)}, u32[]{:S(2)}, u32[]{:S(2)}) collective-permute-start(f32[264,128]{1,0:T(8,128)S(1)} %get-tuple-element.28), channel_id=1, source_target_pairs={{252,32},{0,4},{4,8},{8,12},{12,16},{16,20},{20,24},{24,28},{28,64... | collective-permute-start | bytes 405512 | tf_op jit(solution)/shard_map/ppermute | solution.py:410
  177.2 14.8 %copy-start.5 = (f32[264,128]{1,0:T(8,128)}, f32[264,128]{1,0:T(8,128)S(1)}, u32[]{:S(2)}) copy-start(f32[264,128]{1,0:T(8,128)S(1)} %collective-permute-done.8.refs_5_) | copy-start | bytes 405508
  177.2 14.8 %collective-permute-start.3 = (f32[264,128]{1,0:T(8,128)S(1)}, f32[264,128]{1,0:T(8,128)S(1)}, u32[]{:S(2)}, u32[]{:S(2)}) collective-permute-start(f32[264,128]{1,0:T(8,128)S(1)} %get-tuple-element.29), channel_id=1, source_target_pairs={{252,28},{0,32},{4,4},{8,8},{12,12},{16,16},{20,20},{24,24},{28,60... | collective-permute-start | bytes 405512 | tf_op jit(solution)/shard_map/ppermute | solution.py:410
  179.2 12.9 %copy-start.6 = (f32[264,128]{1,0:T(8,128)}, f32[264,128]{1,0:T(8,128)S(1)}, u32[]{:S(2)}) copy-start(f32[264,128]{1,0:T(8,128)S(1)} %collective-permute-done.7.refs_4_) | copy-start | bytes 405508
  186.0 6.1 %copy-start.7 = (f32[264,128]{1,0:T(8,128)}, f32[264,128]{1,0:T(8,128)S(1)}, u32[]{:S(2)}) copy-start(f32[264,128]{1,0:T(8,128)S(1)} %collective-permute-done.6.refs_3_) | copy-start | bytes 405508
  186.0 6.1 %copy-start.8 = (f32[264,128]{1,0:T(8,128)}, f32[264,128]{1,0:T(8,128)S(1)}, u32[]{:S(2)}) copy-start(f32[264,128]{1,0:T(8,128)S(1)} %collective-permute-done.5.refs_2_) | copy-start | bytes 405508
  192.0 0.7 copy-start.9
  192.7 0.7 copy-start.10
